TPU v7x, 32 devices: a whole 2x2x4 slice. The times are simulated.
32 devices in a mesh: row: 4 (over y, x), col: 8 (over z, core).
Axes of the slice: x: 2, y: 2, z: 4, core: 2. Of those that a mesh axis runs over, the one named last changes fastest.
Arguments:
- x_slab: bfloat16 [8, 16, 64, 128], P('row', 'col'), may hold values from -220 to 220
- h_blocks: bfloat16 [8, 16, 25, 4096], P('row', 'col'), may hold values from -0.21875 to 0.21875
- h_cols: int32 [8, 16, 25], P('row', 'col'), may hold values from 0 to 127, as said below
- h_count: int32 [8, 16], P('row', 'col'), may hold values from 1 to 25, as said below
- z_blocks: bfloat16 [8, 16, 25, 4096], P('row', 'col'), may hold values from -0.15625 to 0.15625
- z_cols: int32 [8, 16, 25], P('row', 'col'), may hold values from 0 to 127, as said below
- z_count: int32 [8, 16], P('row', 'col'), may hold values from 1 to 25, as said below
Outputs:
- cheb_one: bfloat16 [8, 16, 64, 128], P('row', 'col')
- cheb_two: bfloat16 [8, 16, 64, 128], P('row', 'col')
Inputs may be any that keep to these rules, and one draw needn't show every extreme that they name: `h_cols`: the 25 entries of a block cell name the 25 distinct cells within 2 cells of it along each lattice dimension, the lattice being periodic; only the first h_count entries of a cell are live, the others are padding. `h_count`: some cell has 25 live entries and some cell has 1. `z_cols`: the 25 entries of a block cell name the 25 distinct cells within 2 cells of it along each lattice dimension, the lattice being periodic; only the first z_count entries of a cell are live, the others are padding. `z_count`: some cell has 25 live entries and some cell has 1.
All inputs are finite; a program needn't handle non-finite values.
Results may differ from a plain program's by a relative error of at most 0.0085.
Values may be sent and summed in bfloat16 or wider, within the bound.
A program may use at most 64 MiB of HBM per device.

v0:
```python
import functools

import jax
import jax.numpy as jnp
from jax import lax
from jax.experimental import pallas as pl
from jax.experimental.pallas import tpu as pltpu
from jax.sharding import PartitionSpec as P

MESH = pl.DeviceIdType.MESH
STEPS = 6
HALVES = 1
OWN = (0, 0)
FIRST = (
    (((-1, 0), (-1, 0)), ((1, 0), (1, 0)), ((1, -1), (1, -1)), ((0, -1), (0, -1)), ((0, 1), (0, 1))),
    (((-1, 0), (-1, 0)), ((1, 0), (1, 0)), ((1, -1), (1, -1)), ((0, -1), (0, -1)), ((0, 1), (0, 1))),
)
NEXT = (
    (((-1, 0), (0, -1), (-1, -1)), ((1, 0), (0, 1), (1, 1)), ((-1, 0), (0, 1), (-1, 1))),
    (((-1, 0), (0, -1), (-1, -1)), ((1, 0), (0, 1), (1, 1)), ((-1, 0), (0, 1), (-1, 1))),
)
ORDER = (
    ((0, 1), (1, 0), (-1, 0), (0, -1), (1, 1), (-1, 1), (1, -1), (-1, -1)),
    ((0, 1), (1, 0), (-1, 0), (0, -1), (1, 1), (-1, 1), (1, -1), (-1, -1)),
)
LATE = 2


def slot_of(alpha, beta):
    return (alpha + 1) * 3 + beta + 1


def kernel(rows, cols, side, block,
           x_ref, zb_hbm, zc_ref, zn_ref, hb_hbm, hc_ref, hn_ref,
           one_ref, two_ref,
           *scratch):
    bufs = [scratch[HALVES * step:HALVES * (step + 1)] for step in range(STEPS)]
    (z_raw, h_raw, spread, pair_tmp, z_wide, h_wide, power_ref, col_part, row_part,
     load_sem, send_sem, recv_sem, csend, crecv, rsend, rrecv) = scratch[HALVES * STEPS:]
    r = lax.axis_index("row")
    c = lax.axis_index("col")
    s = 1 - 2 * lax.rem(r, 2)
    t = 1 - 2 * lax.rem(c, 2)
    cells = side * side
    slots = 9
    total = slots * cells
    pitch = spread.shape[0] // (block // 2)

    def at(alpha, beta):
        return (lax.rem(r + alpha * s + rows, rows), lax.rem(c + beta * t + cols, cols))

    z_load = pltpu.make_async_copy(zb_hbm, z_raw, load_sem.at[0])
    h_load = pltpu.make_async_copy(hb_hbm, h_raw, load_sem.at[1])
    z_load.start()
    h_load.start()

    barrier = pltpu.get_barrier_semaphore()
    greeted = 0
    for alpha in (-1, 0, 1):
        for beta in (-1, 0, 1):
            if alpha or beta:
                pl.semaphore_signal(barrier, inc=1, device_id=at(alpha, beta), device_id_type=MESH)
                greeted += 1
    for d in range(2, cols - 1):
        pl.semaphore_signal(barrier, inc=1, device_id=(r, lax.rem(c + d, cols)), device_id_type=MESH)
        greeted += 1
    for d in range(2, rows - 1):
        pl.semaphore_signal(barrier, inc=1, device_id=(lax.rem(r + d, rows), c), device_id_type=MESH)
        greeted += 1
    pl.semaphore_wait(barrier, greeted)

    def send(step, part, source, device, target):
        place = slot_of(*target)
        copy = pltpu.make_async_remote_copy(
            src_ref=bufs[step][part].at[slot_of(*source)],
            dst_ref=bufs[step][part].at[place],
            send_sem=send_sem.at[step, part, place],
            recv_sem=recv_sem.at[step, part, place],
            device_id=at(*device),
            device_id_type=MESH,
        )
        copy.start()
        return copy

    def begin(step, part):
        return {target: send(step, part, OWN, device, target) for device, target in FIRST[part]}

    flying = {}
    landed = set()

    def arrive(step, part, where):
        if (step, part, where) not in landed:
            landed.add((step, part, where))
            flights = flying[step, part]
            flights[where].wait_recv()
            for source, device, target in NEXT[part]:
                if source == where:
                    flights[target] = send(step, part, source, device, target)

    def relay(step, part):
        for source, _, _ in NEXT[part]:
            arrive(step, part, source)

    def finish(step, part, other, wide):
        buf = bufs[step][part]

        def product(where):
            slot = slot_of(*where)
            value = buf[slot]
            return jnp.dot(wide[slot], value, preferred_element_type=jnp.float32)

        acc = product(OWN)
        relay(step, part)
        for count, where in enumerate(ORDER[part]):
            if count == len(ORDER[part]) - LATE and other in flying:
                relay(*other)
            arrive(step, part, where)
            acc = acc + product(where)
        return acc

    def drain(flights):
        for copy in flights.values():
            copy.wait_send()

    def targets(width):
        place = lax.broadcasted_iota(jnp.int32, (pitch, width), 0)
        wanted = jnp.full((pitch, width), -1, jnp.int32)
        for alpha in (-1, 0, 1):
            for beta in (-1, 0, 1):
                row_at, col_at = at(alpha, beta)
                for cell in range(cells):
                    number = (row_at * side + cell // side) * (cols * side) + col_at * side + cell % side
                    wanted = jnp.where(place == slot_of(alpha, beta) * cells + cell, number, wanted)
        return wanted

    entries = z_raw.shape[1]
    area = z_raw.shape[2]
    half = block // 2
    pair = 2 * block
    wanted = targets(entries)
    entry = lax.broadcasted_iota(jnp.int32, (pitch, entries), 1)
    low = lax.broadcasted_iota(jnp.int32, (half, pair), 1) < block
    chunk = 4 * pair

    def arrange(raw, col_ref, count_ref, wide):
        for cell in range(cells):
            cy, cx = cell // side, cell % side
            named = col_ref[cy, cx:cx + 1, :]
            picked = (named == wanted) & (entry < count_ref[cy, cx])
            chooser = jnp.where(picked, 1.0, 0.0).astype(jnp.bfloat16)

            for part in range(area // chunk):
                got = jnp.dot(chooser, raw[cell, :, part * chunk:(part + 1) * chunk],
                              preferred_element_type=jnp.float32)
                for piece in range(chunk // pair):
                    line = part * (chunk // pair) + piece
                    spread[line * pitch:(line + 1) * pitch, :] = got[:, piece * pair:(piece + 1) * pair]

            def one_slot(slot, _):
                for duo in range(cells // 2):
                    first = spread[pl.ds(slot * cells + 2 * duo, half, stride=pitch), :]
                    second = spread[pl.ds(slot * cells + 2 * duo + 1, half, stride=pitch), :]
                    pair_tmp[duo, pl.ds(0, half, stride=2), :] = jnp.where(low, first, pltpu.roll(second, block, 1))
                    pair_tmp[duo, pl.ds(1, half, stride=2), :] = jnp.where(low, pltpu.roll(first, block, 1), second)
                for duo in range(cells // 2):
                    wide[slot, cell * block:(cell + 1) * block, duo * pair:(duo + 1) * pair] = (
                        pair_tmp[duo].astype(jnp.bfloat16))
                return 0

            lax.fori_loop(0, slots, one_slot, 0)

    tall, width = x_ref.shape
    middle, halfway = tall // 2, width // 2
    left = lax.broadcasted_iota(jnp.int32, (middle, width), 1) < halfway
    own = slot_of(*OWN)

    def packed(value):
        return (value,)

    def unpacked(ref, parts):
        ref[...] = parts[0].astype(ref.dtype)

    both = range(HALVES)
    x_float = x_ref[...].astype(jnp.float32)
    for part, value in enumerate(packed(x_float)):
        bufs[0][part][own] = value.astype(jnp.bfloat16)
        flying[0, part] = begin(0, part)

    def advance(step, part, wide, root):
        other = (step, part + 1) if part + 1 < HALVES else (step + 1, 0)
        value = finish(step, part, other, wide)
        if root:
            value = bufs[step][part][own].astype(jnp.float32) + value
        if step + 1 < STEPS:
            bufs[step + 1][part][own] = value.astype(jnp.bfloat16)
            flying[step + 1, part] = begin(step + 1, part)
        return value

    z_load.wait()
    arrange(z_raw, zc_ref, zn_ref, z_wide)
    for part in both:
        advance(0, part, z_wide, True)
    h_load.wait()
    arrange(h_raw, hc_ref, hn_ref, h_wide)
    for part in both:
        advance(1, part, h_wide, False)
    x_square = jnp.sum(x_float * x_float, axis=0, keepdims=True)
    power_square = jnp.zeros((1, width), jnp.float32)
    for part in both:
        power = advance(2, part, z_wide, True)
        power_ref[part] = power
        power_square = power_square + jnp.sum(power * power, axis=0, keepdims=True)
    line_id = lax.broadcasted_iota(jnp.int32, col_part.shape[1:], 0)
    col_part[0] = jnp.where(line_id == 0, power_square, jnp.where(line_id == 1, x_square, 0.0))

    def gather_start(part, count, peer, ssem, rsem):
        copies = []
        for d in range(1, count):
            copy = pltpu.make_async_remote_copy(
                src_ref=part.at[0],
                dst_ref=part.at[d],
                send_sem=ssem.at[d],
                recv_sem=rsem.at[d],
                device_id=peer(d),
                device_id_type=MESH,
            )
            copy.start()
            copies.append(copy)
        return copies

    def gather_sum(part, copies):
        for copy in copies:
            copy.wait()
        return jnp.sum(part[...], axis=0)

    col_copies = gather_start(col_part, cols, lambda d: (r, lax.rem(c + d, cols)), csend, crecv)

    for part in both:
        advance(3, part, z_wide, True)
    row_part[0] = gather_sum(col_part, col_copies)
    row_copies = gather_start(row_part, rows, lambda d: (lax.rem(r + d, rows), c), rsend, rrecv)

    for part in both:
        advance(4, part, h_wide, False)
    sums = jnp.sum(gather_sum(row_part, row_copies), axis=1, keepdims=True)
    scale = jnp.sqrt(sums[0:1] / (sums[1:2] + 1e-06))
    inverse = 1.0 / scale
    unpacked(one_ref, [power_ref[part] / scale for part in both])
    for step in range(STEPS - 1):
        for part in both:
            drain(flying[step, part])

    x_parts = packed(x_float)
    ends = []
    for part in both:
        v_three = advance(5, part, z_wide, True)
        ends.append(2.0 * (v_three * inverse) * inverse - x_parts[part])
    unpacked(two_ref, ends)
    for part in both:
        drain(flying[5, part])


def solution(mesh):
    rows, cols = mesh.shape["row"], mesh.shape["col"]

    def body(x_slab, h_blocks, h_cols, h_count, z_blocks, z_cols, z_count):
        side, _, block, width = x_slab.shape
        entries, area = h_blocks.shape[2:]
        cells = side * side
        tall = cells * block
        pitch = -(-(9 * cells) // 8) * 8
        field = pltpu.VMEM((9, tall // HALVES, width), jnp.bfloat16)
        vmem = pl.BlockSpec(memory_space=pltpu.VMEM)
        smem = pl.BlockSpec(memory_space=pltpu.SMEM)
        hbm = pl.BlockSpec(memory_space=pl.ANY)
        out = jax.ShapeDtypeStruct((tall, width), jnp.bfloat16)
        one, two = pl.pallas_call(
            functools.partial(kernel, rows, cols, side, block),
            out_shape=(out, out),
            in_specs=[vmem, hbm, vmem, smem, hbm, vmem, smem],
            out_specs=(vmem, vmem),
            scratch_shapes=[field] * (STEPS * HALVES) + [
                pltpu.VMEM((cells, entries, area), jnp.bfloat16),
                pltpu.VMEM((cells, entries, area), jnp.bfloat16),
                pltpu.VMEM((block // 2 * pitch, 2 * block), jnp.float32),
                pltpu.VMEM((cells // 2, block, 2 * block), jnp.float32),
                pltpu.VMEM((9, tall, tall), jnp.bfloat16),
                pltpu.VMEM((9, tall, tall), jnp.bfloat16),
                pltpu.VMEM((HALVES, tall // HALVES, width), jnp.float32),
                pltpu.VMEM((cols, 8, width), jnp.float32),
                pltpu.VMEM((rows, 8, width), jnp.float32),
                pltpu.SemaphoreType.DMA((2,)),
                pltpu.SemaphoreType.DMA((STEPS, HALVES, 9)),
                pltpu.SemaphoreType.DMA((STEPS, HALVES, 9)),
                pltpu.SemaphoreType.DMA((cols,)),
                pltpu.SemaphoreType.DMA((cols,)),
                pltpu.SemaphoreType.DMA((rows,)),
                pltpu.SemaphoreType.DMA((rows,)),
            ],
            compiler_params=pltpu.CompilerParams(
                collective_id=0, has_side_effects=True, vmem_limit_bytes=40 * 1024 * 1024
            ),
            name="cheb",
        )(
            x_slab.reshape(tall, width),
            z_blocks.reshape(cells, entries, area), z_cols, z_count,
            h_blocks.reshape(cells, entries, area), h_cols, h_count,
        )
        return one.reshape(x_slab.shape), two.reshape(x_slab.shape)

    grid4 = P("row", "col", None, None)
    grid3 = P("row", "col", None)
    in_specs = (grid4, grid4, grid3, P("row", "col"), grid4, grid3, P("row", "col"))
    return jax.shard_map(body, mesh=mesh, in_specs=in_specs, out_specs=(grid4, grid4), check_vma=False)
```

profile of v0, /device:TPU:0, one launch (start us, length us, event | category | flops | bytes accessed | tf_op | source)
XLA Modules:
  0.0 63.5 jit_solution(13741776085981911747)
XLA Ops:
  0.6 0.0 copy-start.5
  0.6 1.7 %copy.10 = bf16[2,2,25,4096]{3,2,1,0:T(8,128)(2,1)S(1)} copy(bf16[2,2,25,4096]{3,1,2,0:T(2,128)(2,1)} %param.8) | data formatting | bytes 1638400 | tf_op args[1]
  2.3 0.0 copy-done.5
  2.3 0.0 copy-start
  2.4 0.0 copy-start.1
  2.4 0.0 copy-start.2
  2.4 0.0 copy-start.4
  2.4 0.5 copy.9
  2.9 0.0 copy-start.3
  2.9 0.3 copy-done
  3.2 0.0 copy-done.1
  3.2 0.0 copy-done.2
  3.2 0.0 copy-done.4
  3.2 0.4 copy-done.3
  3.5 58.7 %cheb.1 = (bf16[256,128]{1,0:T(8,128)(2,1)S(1)}, bf16[256,128]{1,0:T(8,128)(2,1)S(1)}) custom-call(bf16[256,128]{1,0:T(8,128)(2,1)S(1)} %bitcast.7, bf16[4,25,4096]{2,1,0:T(8,128)(2,1)S(1)} %bitcast.6, s32[2,2,25]{2,1,0:T(2,128)S(1)} %copy-done.1, s32[2,2]{1,0:T(2,128)S(1)} %copy-done.3, bf16[4,25,4096]{2,1,0:T(8,128)(2,1)S(1)} %bitcast.5, ...), custom_call_target="tpu_custom_call" | custom-call | tf_op jit(solution)/shard_map/cheb/pallas_call | solution.py:277
  62.3 0.6 copy.13
  62.9 0.6 copy.14
Async XLA Ops:
  0.6 1.7 %copy-start.5 = (bf16[2,2,25,4096]{3,1,2,0:T(2,128)(2,1)S(1)}, bf16[2,2,25,4096]{3,1,2,0:T(2,128)(2,1)}, u32[]{:S(2)}) copy-start(bf16[2,2,25,4096]{3,1,2,0:T(2,128)(2,1)} %param.11) | copy-start | bytes 2457604
  2.3 0.8 %copy-start = (bf16[2,2,64,128]{3,2,1,0:T(8,128)(2,1)S(1)}, bf16[2,2,64,128]{3,2,1,0:T(8,128)(2,1)}, u32[]{:S(2)}) copy-start(bf16[2,2,64,128]{3,2,1,0:T(8,128)(2,1)} %param.7) | copy-start | bytes 196612
  2.4 0.8 %copy-start.1 = (s32[2,2,25]{2,1,0:T(2,128)S(1)}, s32[2,2,25]{2,1,0:T(2,128)}, u32[]{:S(2)}) copy-start(s32[2,2,25]{2,1,0:T(2,128)} %zc_ref.1) | copy-start | bytes 1204
  2.4 0.8 %copy-start.2 = (s32[2,2,25]{2,1,0:T(2,128)S(1)}, s32[2,2,25]{2,1,0:T(2,128)}, u32[]{:S(2)}) copy-start(s32[2,2,25]{2,1,0:T(2,128)} %hc_ref.1) | copy-start | bytes 1204
  2.4 0.8 %copy-start.4 = (s32[2,2]{1,0:T(2,128)S(1)}, s32[2,2]{1,0:T(2,128)}, u32[]{:S(2)}) copy-start(s32[2,2]{1,0:T(2,128)} %hn_ref.1) | copy-start | bytes 52
  2.9 0.7 %copy-start.3 = (s32[2,2]{1,0:T(2,128)S(1)}, s32[2,2]{1,0:T(2,128)}, u32[]{:S(2)}) copy-start(s32[2,2]{1,0:T(2,128)} %zn_ref.1) | copy-start | bytes 52
where the time goes:
time: 63.7 us; the launch traced here: 63.5 us
  Pallas kernels  58.7 us (92%)
  local copies, waits for them, and re-layouts  4.11 us (6%)
  between operations  0.71 us (1%)
    pallas_call x1, Pallas kernels, body(): pl.pallas_call(functools.partial(kernel, rows, cols, side, block), out_sh...  58.7 us
    unnamed x16, local copies, waits for them, and re-layouts  4.11 us

commit v1 on v0

--- a/solution.py
+++ b/solution.py
@@ -9,21 +9,11 @@
 
 MESH = pl.DeviceIdType.MESH
 STEPS = 6
-HALVES = 1
+HALVES = 2
 OWN = (0, 0)
-FIRST = (
-    (((-1, 0), (-1, 0)), ((1, 0), (1, 0)), ((1, -1), (1, -1)), ((0, -1), (0, -1)), ((0, 1), (0, 1))),
-    (((-1, 0), (-1, 0)), ((1, 0), (1, 0)), ((1, -1), (1, -1)), ((0, -1), (0, -1)), ((0, 1), (0, 1))),
-)
-NEXT = (
-    (((-1, 0), (0, -1), (-1, -1)), ((1, 0), (0, 1), (1, 1)), ((-1, 0), (0, 1), (-1, 1))),
-    (((-1, 0), (0, -1), (-1, -1)), ((1, 0), (0, 1), (1, 1)), ((-1, 0), (0, 1), (-1, 1))),
-)
-ORDER = (
-    ((0, 1), (1, 0), (-1, 0), (0, -1), (1, 1), (-1, 1), (1, -1), (-1, -1)),
-    ((0, 1), (1, 0), (-1, 0), (0, -1), (1, 1), (-1, 1), (1, -1), (-1, -1)),
-)
-LATE = 2
+FIRST = ((0, -1), (-1, -1), (1, -1), (-1, 0), (1, 0), (0, 1))
+NEXT = (((-1, 0), (0, 1), (-1, 1)), ((1, 0), (0, 1), (1, 1)))
+GROUPS = ((OWN,), ((-1, 0), (1, 0), (0, 1), (0, -1)), ((1, -1), (-1, -1)), ((-1, 1), (1, 1)))
 
 
 def slot_of(alpha, beta):
@@ -42,6 +32,8 @@
     s = 1 - 2 * lax.rem(r, 2)
     t = 1 - 2 * lax.rem(c, 2)
     cells = side * side
+    tall, width = x_ref.shape
+    middle, halfway = tall // 2, width // 2
     slots = 9
     total = slots * cells
     pitch = spread.shape[0] // (block // 2)
@@ -83,7 +75,7 @@
         return copy
 
     def begin(step, part):
-        return {target: send(step, part, OWN, device, target) for device, target in FIRST[part]}
+        return {target: send(step, part, OWN, target, target) for target in FIRST}
 
     flying = {}
     landed = set()
@@ -93,29 +85,26 @@
             landed.add((step, part, where))
             flights = flying[step, part]
             flights[where].wait_recv()
-            for source, device, target in NEXT[part]:
+            for source, device, target in NEXT:
                 if source == where:
                     flights[target] = send(step, part, source, device, target)
 
-    def relay(step, part):
-        for source, _, _ in NEXT[part]:
-            arrive(step, part, source)
-
-    def finish(step, part, other, wide):
+    def finish(step, part, wide):
         buf = bufs[step][part]
 
         def product(where):
             slot = slot_of(*where)
             value = buf[slot]
+            value = jnp.concatenate([value, pltpu.roll(value, halfway, 1)], axis=0)
             return jnp.dot(wide[slot], value, preferred_element_type=jnp.float32)
 
-        acc = product(OWN)
-        relay(step, part)
-        for count, where in enumerate(ORDER[part]):
-            if count == len(ORDER[part]) - LATE and other in flying:
-                relay(*other)
-            arrive(step, part, where)
-            acc = acc + product(where)
+        acc = None
+        for group in GROUPS:
+            for where in group:
+                if where != OWN:
+                    arrive(step, part, where)
+            for where in group:
+                acc = product(where) if acc is None else acc + product(where)
         return acc
 
     def drain(flights):
@@ -169,16 +158,23 @@
 
             lax.fori_loop(0, slots, one_slot, 0)
 
-    tall, width = x_ref.shape
-    middle, halfway = tall // 2, width // 2
     left = lax.broadcasted_iota(jnp.int32, (middle, width), 1) < halfway
     own = slot_of(*OWN)
 
+    def turn(value):
+        return pltpu.roll(value, halfway, 1)
+
     def packed(value):
-        return (value,)
+        top, low_rows = value[:middle], value[middle:]
+        return (jnp.where(left, top, turn(low_rows)), jnp.where(left, turn(top), low_rows))
+
+    def folded(value):
+        return jnp.where(left, value[:middle], turn(value[middle:]))
 
     def unpacked(ref, parts):
-        ref[...] = parts[0].astype(ref.dtype)
+        first, second = parts
+        ref[:middle] = jnp.where(left, first, turn(second)).astype(ref.dtype)
+        ref[middle:] = jnp.where(left, turn(first), second).astype(ref.dtype)
 
     both = range(HALVES)
     x_float = x_ref[...].astype(jnp.float32)
@@ -187,8 +183,7 @@
         flying[0, part] = begin(0, part)
 
     def advance(step, part, wide, root):
-        other = (step, part + 1) if part + 1 < HALVES else (step + 1, 0)
-        value = finish(step, part, other, wide)
+        value = folded(finish(step, part, wide))
         if root:
             value = bufs[step][part][own].astype(jnp.float32) + value
         if step + 1 < STEPS:

time: 63.7 us -> 58.3 us (0.915)
  Pallas kernels: 58.7 us -> 53.3 us
    pallas_call x1, Pallas kernels: 58.7 us -> 53.3 us  [body(): pl.pallas_call(functools.partial(kernel, rows, cols, side, block), out_sh...]
where the time goes in v1:
time: 58.3 us; the launch traced here: 58.1 us
  Pallas kernels  53.3 us (91%)
  local copies, waits for them, and re-layouts  4.11 us (7%)
  between operations  0.71 us (1%)
    pallas_call x1, Pallas kernels, body(): pl.pallas_call(functools.partial(kernel, rows, cols, side, block), out_sh...  53.3 us
    unnamed x16, local copies, waits for them, and re-layouts  4.11 us

profile of v1, /device:TPU:0, one launch (start us, length us, event | category | flops | bytes accessed | tf_op | source)
XLA Modules:
  0.0 58.1 jit_solution(1916052171497096557)
XLA Ops:
  0.6 0.0 copy-start.5
  0.6 1.7 %copy.10 = bf16[2,2,25,4096]{3,2,1,0:T(8,128)(2,1)S(1)} copy(bf16[2,2,25,4096]{3,1,2,0:T(2,128)(2,1)} %param.8) | data formatting | bytes 1638400 | tf_op args[1]
  2.3 0.0 copy-done.5
  2.3 0.0 copy-start
  2.4 0.0 copy-start.1
  2.4 0.0 copy-start.2
  2.4 0.0 copy-start.4
  2.4 0.5 copy.9
  2.9 0.0 copy-start.3
  2.9 0.3 copy-done
  3.2 0.0 copy-done.1
  3.2 0.0 copy-done.2
  3.2 0.0 copy-done.4
  3.2 0.4 copy-done.3
  3.5 53.3 %cheb.1 = (bf16[256,128]{1,0:T(8,128)(2,1)S(1)}, bf16[256,128]{1,0:T(8,128)(2,1)S(1)}) custom-call(bf16[256,128]{1,0:T(8,128)(2,1)S(1)} %bitcast.7, bf16[4,25,4096]{2,1,0:T(8,128)(2,1)S(1)} %bitcast.6, s32[2,2,25]{2,1,0:T(2,128)S(1)} %copy-done.1, s32[2,2]{1,0:T(2,128)S(1)} %copy-done.3, bf16[4,25,4096]{2,1,0:T(8,128)(2,1)S(1)} %bitcast.5, ...), custom_call_target="tpu_custom_call" | custom-call | tf_op jit(solution)/shard_map/cheb/pallas_call | solution.py:272
  56.9 0.6 %copy.13 = bf16[2,2,64,128]{3,2,1,0:T(8,128)(2,1)} copy(bf16[2,2,64,128]{3,2,1,0:T(8,128)(2,1)S(1)} %bitcast.9) | data formatting | bytes 131072
  57.5 0.6 %copy.14 = bf16[2,2,64,128]{3,2,1,0:T(8,128)(2,1)} copy(bf16[2,2,64,128]{3,2,1,0:T(8,128)(2,1)S(1)} %bitcast.8) | data formatting | bytes 131072
Async XLA Ops:
  0.6 1.7 %copy-start.5 = (bf16[2,2,25,4096]{3,1,2,0:T(2,128)(2,1)S(1)}, bf16[2,2,25,4096]{3,1,2,0:T(2,128)(2,1)}, u32[]{:S(2)}) copy-start(bf16[2,2,25,4096]{3,1,2,0:T(2,128)(2,1)} %param.11) | copy-start | bytes 2457604
  2.3 0.8 %copy-start = (bf16[2,2,64,128]{3,2,1,0:T(8,128)(2,1)S(1)}, bf16[2,2,64,128]{3,2,1,0:T(8,128)(2,1)}, u32[]{:S(2)}) copy-start(bf16[2,2,64,128]{3,2,1,0:T(8,128)(2,1)} %param.7) | copy-start | bytes 196612
  2.4 0.8 %copy-start.1 = (s32[2,2,25]{2,1,0:T(2,128)S(1)}, s32[2,2,25]{2,1,0:T(2,128)}, u32[]{:S(2)}) copy-start(s32[2,2,25]{2,1,0:T(2,128)} %zc_ref.1) | copy-start | bytes 1204
  2.4 0.8 %copy-start.2 = (s32[2,2,25]{2,1,0:T(2,128)S(1)}, s32[2,2,25]{2,1,0:T(2,128)}, u32[]{:S(2)}) copy-start(s32[2,2,25]{2,1,0:T(2,128)} %hc_ref.1) | copy-start | bytes 1204
  2.4 0.8 %copy-start.4 = (s32[2,2]{1,0:T(2,128)S(1)}, s32[2,2]{1,0:T(2,128)}, u32[]{:S(2)}) copy-start(s32[2,2]{1,0:T(2,128)} %hn_ref.1) | copy-start | bytes 52
  2.9 0.7 %copy-start.3 = (s32[2,2]{1,0:T(2,128)S(1)}, s32[2,2]{1,0:T(2,128)}, u32[]{:S(2)}) copy-start(s32[2,2]{1,0:T(2,128)} %zn_ref.1) | copy-start | bytes 52

commit v2 on v1

--- a/solution.py
+++ b/solution.py
@@ -13,7 +13,7 @@
 OWN = (0, 0)
 FIRST = ((0, -1), (-1, -1), (1, -1), (-1, 0), (1, 0), (0, 1))
 NEXT = (((-1, 0), (0, 1), (-1, 1)), ((1, 0), (0, 1), (1, 1)))
-GROUPS = ((OWN,), ((-1, 0), (1, 0), (0, 1), (0, -1)), ((1, -1), (-1, -1)), ((-1, 1), (1, 1)))
+GROUPS = (((-1, 0), (1, 0), (0, 1), (0, -1), OWN), ((1, -1), (-1, -1), (-1, 1), (1, 1)))
 
 
 def slot_of(alpha, beta):
@@ -89,6 +89,10 @@
                 if source == where:
                     flights[target] = send(step, part, source, device, target)
 
+    def relay(step, part):
+        for source, _, _ in NEXT:
+            arrive(step, part, source)
+
     def finish(step, part, wide):
         buf = bufs[step][part]
 
@@ -131,8 +135,8 @@
     low = lax.broadcasted_iota(jnp.int32, (half, pair), 1) < block
     chunk = 4 * pair
 
-    def arrange(raw, col_ref, count_ref, wide):
-        for cell in range(cells):
+    def arrange(raw, col_ref, count_ref, wide, first, last):
+        for cell in range(first, last):
             cy, cx = cell // side, cell % side
             named = col_ref[cy, cx:cx + 1, :]
             picked = (named == wanted) & (entry < count_ref[cy, cx])
@@ -192,11 +196,15 @@
         return value
 
     z_load.wait()
-    arrange(z_raw, zc_ref, zn_ref, z_wide)
-    for part in both:
-        advance(0, part, z_wide, True)
+    arrange(z_raw, zc_ref, zn_ref, z_wide, 0, cells)
     h_load.wait()
-    arrange(h_raw, hc_ref, hn_ref, h_wide)
+    early = cells // 4
+    arrange(h_raw, hc_ref, hn_ref, h_wide, 0, early)
+    relay(0, 0)
+    arrange(h_raw, hc_ref, hn_ref, h_wide, early, 2 * early)
+    advance(0, 0, z_wide, True)
+    arrange(h_raw, hc_ref, hn_ref, h_wide, 2 * early, cells)
+    advance(0, 1, z_wide, True)
     for part in both:
         advance(1, part, h_wide, False)
     x_square = jnp.sum(x_float * x_float, axis=0, keepdims=True)
@@ -241,18 +249,14 @@
     scale = jnp.sqrt(sums[0:1] / (sums[1:2] + 1e-06))
     inverse = 1.0 / scale
     unpacked(one_ref, [power_ref[part] / scale for part in both])
-    for step in range(STEPS - 1):
-        for part in both:
-            drain(flying[step, part])
-
     x_parts = packed(x_float)
     ends = []
     for part in both:
         v_three = advance(5, part, z_wide, True)
         ends.append(2.0 * (v_three * inverse) * inverse - x_parts[part])
     unpacked(two_ref, ends)
-    for part in both:
-        drain(flying[5, part])
+    for flights in flying.values():
+        drain(flights)
 
 
 def solution(mesh):

time: 58.3 us -> 57.5 us (0.986)
  Pallas kernels: 53.3 us -> 52.2 us
    pallas_call x1, Pallas kernels: 53.3 us -> 52.2 us  [body(): pl.pallas_call(functools.partial(kernel, rows, cols, side, block), out_sh...]
where the time goes in v2:
time: 57.5 us; the launch traced here: 57 us
  Pallas kernels  52.2 us (91%)
  local copies, waits for them, and re-layouts  4.11 us (7%)
  between operations  0.71 us (1%)
    pallas_call x1, Pallas kernels, body(): pl.pallas_call(functools.partial(kernel, rows, cols, side, block), out_sh...  52.2 us
    unnamed x16, local copies, waits for them, and re-layouts  4.11 us

profile of v2, /device:TPU:0, one launch (start us, length us, event | category | flops | bytes accessed | tf_op | source)
XLA Modules:
  0.0 57.0 jit_solution(12914947897120917142)
XLA Ops:
  0.6 0.0 copy-start.5
  0.6 1.7 %copy.10 = bf16[2,2,25,4096]{3,2,1,0:T(8,128)(2,1)S(1)} copy(bf16[2,2,25,4096]{3,1,2,0:T(2,128)(2,1)} %param.8) | data formatting | bytes 1638400 | tf_op args[1]
  2.3 0.0 copy-done.5
  2.3 0.0 copy-start
  2.4 0.0 copy-start.1
  2.4 0.0 copy-start.2
  2.4 0.0 copy-start.4
  2.4 0.5 copy.9
  2.9 0.0 copy-start.3
  2.9 0.3 copy-done
  3.2 0.0 copy-done.1
  3.2 0.0 copy-done.2
  3.2 0.0 copy-done.4
  3.2 0.4 copy-done.3
  3.5 52.2 %cheb.1 = (bf16[256,128]{1,0:T(8,128)(2,1)S(1)}, bf16[256,128]{1,0:T(8,128)(2,1)S(1)}) custom-call(bf16[256,128]{1,0:T(8,128)(2,1)S(1)} %bitcast.7, bf16[4,25,4096]{2,1,0:T(8,128)(2,1)S(1)} %bitcast.6, s32[2,2,25]{2,1,0:T(2,128)S(1)} %copy-done.1, s32[2,2]{1,0:T(2,128)S(1)} %copy-done.3, bf16[4,25,4096]{2,1,0:T(8,128)(2,1)S(1)} %bitcast.5, ...), custom_call_target="tpu_custom_call" | custom-call | tf_op jit(solution)/shard_map/cheb/pallas_call | solution.py:276
  55.7 0.6 %copy.13 = bf16[2,2,64,128]{3,2,1,0:T(8,128)(2,1)} copy(bf16[2,2,64,128]{3,2,1,0:T(8,128)(2,1)S(1)} %bitcast.9) | data formatting | bytes 131072
  56.4 0.6 %copy.14 = bf16[2,2,64,128]{3,2,1,0:T(8,128)(2,1)} copy(bf16[2,2,64,128]{3,2,1,0:T(8,128)(2,1)S(1)} %bitcast.8) | data formatting | bytes 131072
Async XLA Ops:
  0.6 1.7 %copy-start.5 = (bf16[2,2,25,4096]{3,1,2,0:T(2,128)(2,1)S(1)}, bf16[2,2,25,4096]{3,1,2,0:T(2,128)(2,1)}, u32[]{:S(2)}) copy-start(bf16[2,2,25,4096]{3,1,2,0:T(2,128)(2,1)} %param.11) | copy-start | bytes 2457604
  2.3 0.8 %copy-start = (bf16[2,2,64,128]{3,2,1,0:T(8,128)(2,1)S(1)}, bf16[2,2,64,128]{3,2,1,0:T(8,128)(2,1)}, u32[]{:S(2)}) copy-start(bf16[2,2,64,128]{3,2,1,0:T(8,128)(2,1)} %param.7) | copy-start | bytes 196612
  2.4 0.8 %copy-start.1 = (s32[2,2,25]{2,1,0:T(2,128)S(1)}, s32[2,2,25]{2,1,0:T(2,128)}, u32[]{:S(2)}) copy-start(s32[2,2,25]{2,1,0:T(2,128)} %zc_ref.1) | copy-start | bytes 1204
  2.4 0.8 %copy-start.2 = (s32[2,2,25]{2,1,0:T(2,128)S(1)}, s32[2,2,25]{2,1,0:T(2,128)}, u32[]{:S(2)}) copy-start(s32[2,2,25]{2,1,0:T(2,128)} %hc_ref.1) | copy-start | bytes 1204
  2.4 0.8 %copy-start.4 = (s32[2,2]{1,0:T(2,128)S(1)}, s32[2,2]{1,0:T(2,128)}, u32[]{:S(2)}) copy-start(s32[2,2]{1,0:T(2,128)} %hn_ref.1) | copy-start | bytes 52
  2.9 0.7 %copy-start.3 = (s32[2,2]{1,0:T(2,128)S(1)}, s32[2,2]{1,0:T(2,128)}, u32[]{:S(2)}) copy-start(s32[2,2]{1,0:T(2,128)} %zn_ref.1) | copy-start | bytes 52
